TPU v7x, 128 devices: a whole 4x4x4 slice. The times are simulated.
128 devices in a mesh: wide: 16 (over y, x), narrow: 8 (over z, core).
Axes of the slice: x: 4, y: 4, z: 4, core: 2. Of those that a mesh axis runs over, the one named last changes fastest.
Arguments:
- hidden: bfloat16 [4096, 2048], P(('wide', 'narrow')), may hold values from -6 to 6
- cotangent: bfloat16 [4096, 2048], P(('wide', 'narrow')), may hold values from -6 to 6
- routes: int32 [4096, 6], P(('wide', 'narrow')), may hold values from 0 to 63, all different within a row; in each aligned block of 32 rows (0 to 31, 32 to 63, ...) at most 6 rows name the same one
- gates: float32 [4096, 6], P(('wide', 'narrow')), may hold values from 0.05 to 1
- offsets: int32 [16], replicated, may hold values from 0 to 15, each once
- w_gate: bfloat16 [128, 2048, 704], P(('wide', 'narrow')), may hold values from -0.125 to 0.125
- w_up: bfloat16 [128, 2048, 704], P(('wide', 'narrow')), may hold values from -0.125 to 0.125
- w_down: bfloat16 [128, 704, 2048], P(('wide', 'narrow')), may hold values from -0.15625 to 0.15625
- w_out: bfloat16 [2048, 2048], P('narrow'), may hold values from -0.125 to 0.125
- latent: bfloat16 [4096, 512], P('wide'), may hold values from -6 to 6
- rope_key: bfloat16 [4096, 64], P('wide'), may hold values from -4 to 4
- q_nope: bfloat16 [4096, 2048], P('wide', 'narrow'), may hold values from -24 to 24
- q_pe: bfloat16 [4096, 1024], P('wide', 'narrow'), may hold values from -100 to 100
- w_uk: bfloat16 [2048, 512], P('narrow'), may hold values from -0.5 to 0.5
- w_uv: bfloat16 [2048, 512], P('narrow'), may hold values from -0.5 to 0.5
Outputs:
- resid_grad: bfloat16 [4096, 2048], P(('wide', 'narrow'))
- grad_q_nope: bfloat16 [4096, 2048], P('wide', 'narrow')
- grad_q_pe: bfloat16 [4096, 1024], P('wide', 'narrow')
- grad_latent: float32 [4096, 512], P(('wide', 'narrow'))
- grad_rope_key: float32 [4096, 64], P(('wide', 'narrow'))
Inputs may be any that keep to these rules, and one draw needn't show every extreme that they name: `routes`: each row names 6 different experts; in each aligned block of 32 rows no expert is named by more than 6 rows, and in some blocks one is named by exactly 6. A permutation of the sequence blocks: token i of block b stands at position offsets[b] * 256 + i.
All inputs are finite; a program needn't handle non-finite values.
Results may differ from a plain program's by a relative error of at most 0.028.
Values may be sent and summed in bfloat16 or wider, within the bound.
A program may use at most 128 MiB of HBM per device.

v0:
```python
import functools
import math

import jax
import jax.numpy as jnp
from jax import lax
from jax.experimental import pallas as pl
from jax.experimental.pallas import tpu as pltpu
from jax.sharding import PartitionSpec as P

LATENT = 512
NOPE = 128
ROPE = 64
VDIM = 128
MESH = pl.DeviceIdType.MESH
F32 = jnp.float32
BF16 = jnp.bfloat16
NT = (((1,), (1,)), ((), ()))
NN = (((1,), (0,)), ((), ()))
TN = (((0,), (0,)), ((), ()))


def dot(a, b, dims=NN):
    return lax.dot_general(a, b, dims, preferred_element_type=F32)


def iota(shape, dim):
    return lax.broadcasted_iota(jnp.int32, shape, dim)


def place():
    w = lax.axis_index("wide")
    n = lax.axis_index("narrow")
    return w // 4, w % 4, n // 2, n % 2


def selections(rt, gt):
    expert = iota((512, 32), 0) >> 3
    named = jnp.zeros((512, 32), F32)
    weight = jnp.zeros((512, 32), F32)
    for k in range(6):
        hit = expert == rt[k : k + 1, :]
        named = jnp.where(hit, 1.0, named)
        weight = jnp.where(hit, gt[k : k + 1, :], weight)
    earlier = (iota((32, 32), 0) < iota((32, 32), 1)).astype(F32).astype(BF16)
    before = dot(named.astype(BF16), earlier)
    row = iota((512, 32), 0) & 7
    picks = []
    for j in range(3):
        slot = jnp.where(row < 6, row, jnp.where(row == 6, j, 3 + j))
        picks.append(jnp.where(before == slot.astype(F32), named, 0.0))
    return picks, weight, row


def pack_matrix(j):
    q = iota((192, 256), 1)
    r = iota((192, 256), 0)
    s = q & 7
    base = (q >> 3) * 6
    if j < 0:
        return ((s < 6) & (r == base + s)).astype(F32).astype(BF16)
    return ((s >= 6) & (r == base + (s - 6) * 3 + j)).astype(F32).astype(BF16)


def fold_matrix(j):
    q = iota((256, 192), 0)
    r = iota((256, 192), 1)
    s = q & 7
    base = (q >> 3) * 6
    if j < 0:
        return ((s < 6) & (r == base + s)).astype(F32).astype(BF16)
    return ((s >= 6) & (r == base + (s - 6) * 3 + j)).astype(F32).astype(BF16)


def experts_kernel(
    rt, gt, hid, cot, wg, wu, wd,
    back, comb,
    send, recv, wgb, wub, wdb, xs, dys, acc,
    lsem, ssem, rsem, wssem, wrsem, psem,
):
    y, x, z, c = place()
    me = (y * 4 + x) * 4 + z
    partner = (y * 4 + x, z * 2 + 1 - c)
    bar = pltpu.get_barrier_semaphore()

    def peer(k):
        k = (k * 11) % 64
        pw = ((y + k // 16) % 4) * 4 + (x + (k // 4) % 4) % 4
        pz = (z + k % 4) % 4
        return pw * 4 + pz, (pw, pz * 2 + c)

    def greet(k, _):
        pl.semaphore_signal(bar, inc=1, device_id=peer(k)[1], device_id_type=MESH)
        return 0

    lax.fori_loop(1, 64, greet, 0)
    pl.semaphore_signal(bar, inc=1, device_id=partner, device_id_type=MESH)
    loads = [
        pltpu.make_async_copy(src, dst.at[0], lsem.at[i])
        for i, (src, dst) in enumerate(((wg, wgb), (wu, wub), (wd, wdb)))
    ]
    for q in loads:
        q.start()

    picks, weight, row = selections(rt[...], gt[...])
    cot_hi = cot[:, 1024:2048]
    for j in range(3):
        low = jnp.where(row < 6, picks[j], 0.0).astype(BF16)
        high = jnp.where(row < 6, 0.0, picks[j]).astype(BF16)
        if j == 0:
            comb[0] = low
        comb[1 + j] = high
        part = (hid[:, 0:1024], hid[:, 1024:2048], cot[:, 0:1024])[j]
        gate = jnp.sum(picks[j] * weight, axis=1, keepdims=True)
        if j < 2:
            gate = jnp.where(row[:, 0:1] < 6, 1.0, gate)
        val = (dot(low, part) + dot(high, cot_hi)) * gate
        send[:, :, 1024 * j : 1024 * (j + 1)] = val.astype(BF16).reshape(64, 8, 1024)

    pl.semaphore_wait(bar, 64)

    def out_copy(k):
        pc, dev = peer(k)
        return pltpu.make_async_remote_copy(
            send.at[pc], recv.at[me], ssem.at[pc], rsem.at[me], device_id=dev, device_id_type=MESH
        )

    def in_copy(k):
        pc, dev = peer(k)
        return pltpu.make_async_remote_copy(
            send.at[pc], recv.at[pc], ssem.at[pc], rsem.at[pc], device_id=dev, device_id_type=MESH
        )

    def start(k, _):
        out_copy(k).start()
        return 0

    trades = [
        pltpu.make_async_remote_copy(
            src, dst.at[1], wssem.at[i], wrsem.at[i], device_id=partner, device_id_type=MESH
        )
        for i, (src, dst) in enumerate(((wg, wgb), (wu, wub), (wd, wdb)))
    ]
    lax.fori_loop(1, 64, start, 0)
    for q in trades:
        q.start()
    own = pltpu.make_async_copy(send.at[me], recv.at[me], psem.at[0])
    own.start()
    own.wait()

    def finish(k, _):
        q = in_copy(k)
        q.wait_send()
        q.wait_recv()
        return 0

    lax.fori_loop(1, 64, finish, 0)

    for g in range(2):
        got = recv.at[pl.ds(32 * g, 32)]
        rows = pl.ds(192 * g, 192)
        plain = pack_matrix(-1)

        def cols(a, b):
            return got[:, :, a:b].reshape(256, b - a)

        xs[rows, 0:1024] = dot(plain, cols(0, 1024)).astype(BF16)
        xs[rows, 1024:2048] = dot(plain, cols(1024, 2048)).astype(BF16)
        dys[rows, 0:1024] = dot(plain, cols(2048, 3072)).astype(BF16)
        hi = dot(pack_matrix(0), cols(0, 1024))
        hi = hi + dot(pack_matrix(1), cols(1024, 2048))
        hi = hi + dot(pack_matrix(2), cols(2048, 3072))
        dys[rows, 1024:2048] = hi.astype(BF16)

    for h in range(2):
        if h == 0:
            for q in loads:
                q.wait()
        else:
            for q in trades:
                q.wait()
        pre = dot(xs[...], wgb[h], NT)
        up = dot(xs[...], wub[h], NT)
        gh = dot(dys[...], wdb[h], NT)
        s = jax.nn.sigmoid(pre)
        gg = (gh * up * s * (1.0 + pre * (1.0 - s))).astype(BF16)
        gu = (gh * pre * s).astype(BF16)
        for b in range(2):
            cs = slice(1024 * b, 1024 * (b + 1))
            term = dot(gg, wgb[h, :, cs]) + dot(gu, wub[h, :, cs])
            if h == 0:
                acc[:, cs] = term
            else:
                xs[:, cs] = (acc[:, cs] + term).astype(BF16)

    for g in range(2):
        rows = pl.ds(192 * g, 192)
        plain = fold_matrix(-1)
        for j in range(3):
            val = dot(plain, xs[rows, 512 * j : 512 * (j + 1)])
            val = val + dot(fold_matrix(j), xs[rows, 1536:2048])
            back[32 * g : 32 * (g + 1), :, 512 * j : 512 * (j + 1)] = val.astype(BF16).reshape(32, 8, 512)


def experts(rt, gt, hid, cot, wg, wu, wd):
    vm = pl.BlockSpec(memory_space=pltpu.VMEM)
    hbm = pl.BlockSpec(memory_space=pl.ANY)
    dma = pltpu.SemaphoreType.DMA
    half = wg.shape[0]
    return pl.pallas_call(
        experts_kernel,
        out_shape=(
            jax.ShapeDtypeStruct((64, 8, 1536), BF16),
            jax.ShapeDtypeStruct((4, 512, 32), BF16),
        ),
        in_specs=[vm, vm, vm, vm, hbm, hbm, hbm],
        out_specs=(vm, vm),
        scratch_shapes=[
            pltpu.VMEM((64, 8, 3072), BF16),
            pltpu.VMEM((64, 8, 3072), BF16),
            pltpu.VMEM((2, half, 2048), BF16),
            pltpu.VMEM((2, half, 2048), BF16),
            pltpu.VMEM((2, half, 2048), BF16),
            pltpu.VMEM((384, 2048), BF16),
            pltpu.VMEM((384, 2048), BF16),
            pltpu.VMEM((384, 2048), F32),
            dma((3,)), dma((64,)), dma((64,)), dma((3,)), dma((3,)), dma((1,)),
        ],
        compiler_params=pltpu.CompilerParams(
            collective_id=0, has_side_effects=True, vmem_limit_bytes=62 * 1024 * 1024
        ),
        cost_estimate=pl.CostEstimate(flops=11 * 10**9, bytes_accessed=20 * 10**6, transcendentals=10**6),
    )(rt, gt, hid, cot, wg, wu, wd)


ORDERS = ((2, 0, 1), (0, 1, 2), (1, 2, 0))
CHUNK = 512
CHUNKS = 8
SCALE = 1.0 / math.sqrt(NOPE + ROPE)


def attention_kernel(
    offs, back, comb, cot, keys, qn, qp, wkv, wout,
    own_out, dq_out, dp_out, out,
    landed, gathered, kc, vx, sc, pr, qc, gx, dd,
    terms, r0, a0, r1, a1, r2, a2, r3,
    bssem, brsem, psem, gsem, hsem, s0, t0, ss, rs,
):
    y, x, z, c = place()
    coord = (y, x, z)
    me = (y * 4 + x) * 4 + z
    partner = (y * 4 + x, z * 2 + 1 - c)

    def peer(k):
        k = (k * 11) % 64
        pw = ((y + k // 16) % 4) * 4 + (x + (k // 4) % 4) % 4
        pz = (z + k % 4) % 4
        return pw * 4 + pz, (pw, pz * 2 + c)

    def device(d, o):
        at = list(coord)
        at[d] = (at[d] + o) % 4
        return (at[0] * 4 + at[1], at[2] * 2 + c)

    bar = pltpu.get_barrier_semaphore()

    def greet(k, _):
        pl.semaphore_signal(bar, inc=1, device_id=peer(k)[1], device_id_type=MESH)
        return 0

    lax.fori_loop(1, 64, greet, 0)
    pl.semaphore_signal(bar, inc=1, device_id=partner, device_id_type=MESH)

    zero = jnp.zeros((256, 64), BF16)
    for h in range(2):
        qc[h, :, 0:128] = qn[:, 128 * h : 128 * (h + 1)]
        qc[h, :, 128:256] = jnp.concatenate([qp[:, 64 * h : 64 * (h + 1)], zero], axis=1)

    pl.semaphore_wait(bar, 64)

    def ret_copy(k, at_me):
        pc, dev = peer(k)
        slot = me if at_me else pc
        return pltpu.make_async_remote_copy(
            back.at[pc], landed.at[slot], bssem.at[pc], brsem.at[slot],
            device_id=dev, device_id_type=MESH,
        )

    def ret_start(k, _):
        ret_copy(k, True).start()
        return 0

    lax.fori_loop(1, 64, ret_start, 0)
    own = pltpu.make_async_copy(back.at[me], landed.at[me], psem)
    own.start()

    ones = (iota((CHUNK, 128), 1) < 2).astype(F32).astype(BF16)
    delta = iota((256, 256), 0) - iota((256, 256), 1)
    here = offs[y * 4 + x]

    def forward(i, tops):
        rows = pl.ds(pl.multiple_of(i * CHUNK, CHUNK), CHUNK)
        kv = dot(keys[rows, 0:512], wkv[...], NT).astype(BF16)
        rope = keys[rows, 512:640]
        new = []
        for h in range(2):
            vx[h, rows, 0:128] = kv[:, 128 * h : 128 * (h + 1)]
            vx[h, rows, 128:256] = ones
            kc[h, rows, 0:128] = kv[:, 256 + 128 * h : 256 + 128 * (h + 1)]
            kc[h, rows, 128:256] = rope
            top = tops[h]
            val = dot(kc[h, rows, :], qc[h], NT)
            for b in range(2):
                limit = (here - offs[2 * i + b]) * 256
                part = jnp.where(delta <= limit, val[256 * b : 256 * (b + 1)], -1e30)
                sc[h, pl.ds(pl.multiple_of(i * CHUNK + 256 * b, 256), 256), :] = part
                top = jnp.maximum(top, jnp.max(part.reshape(32, 8, 256), axis=0))
            new.append(top)
        return tuple(new)

    low = jnp.full((8, 256), -1e30, F32)
    tops = lax.fori_loop(0, CHUNKS, forward, (low, low))
    tops = [jnp.max(t, axis=0, keepdims=True) for t in tops]

    def weigh(i, sums):
        rows = pl.ds(pl.multiple_of(i * CHUNK, CHUNK), CHUNK)
        new = []
        for h in range(2):
            p = jnp.exp(SCALE * (sc[h, rows, :] - tops[h])).astype(BF16)
            pr[h, rows, :] = p
            new.append(sums[h] + dot(p, vx[h, rows, :], TN))
        return tuple(new)

    nil = jnp.zeros((256, 256), F32)
    sums = lax.fori_loop(0, CHUNKS, weigh, (nil, nil))

    own.wait()

    def ret_finish(k, _):
        q = ret_copy(k, False)
        q.wait_send()
        q.wait_recv()
        return 0

    lax.fori_loop(1, 64, ret_finish, 0)

    total = cot[...].astype(F32)
    rest = jnp.zeros((32, 512), F32)
    for j in range(3):
        block = landed[:, :, 512 * j : 512 * (j + 1)].reshape(512, 512)
        cs = slice(512 * j, 512 * (j + 1))
        own_out[:, cs] = (total[:, cs] + dot(comb[0], block, TN)).astype(BF16)
        rest = rest + dot(comb[1 + j], block, TN)
    own_out[:, 1536:2048] = (total[:, 1536:2048] + rest).astype(BF16)
    gathered[z, c] = own_out[...]

    hops = []
    for o in range(1, 4):
        pz = (z + o) % 4
        hops.append(
            pltpu.make_async_remote_copy(
                own_out, gathered.at[z, c], gsem.at[o - 1], hsem.at[o - 1],
                device_id=(y * 4 + x, pz * 2 + c), device_id_type=MESH,
            )
        )
    for q in hops:
        q.start()
    for q in hops:
        q.wait()
    last = pltpu.make_async_remote_copy(
        gathered.at[:, c], gathered.at[:, c], gsem.at[3], hsem.at[3], device_id=partner, device_id_type=MESH
    )
    last.start()
    last.wait()

    go = dot(gathered[...].reshape(256, 2048), wout[...], NT).astype(BF16).astype(F32)
    lane = iota((256, 128), 1)
    for h in range(2):
        inv = 1.0 / sums[h][:, 128:129]
        mean = sums[h][:, 0:128] * inv
        scaled = (go[:, 128 * h : 128 * (h + 1)] * inv).astype(BF16)
        drop = -jnp.sum(scaled.astype(F32) * mean, axis=1, keepdims=True)
        high = drop.astype(BF16).astype(F32)
        extra = jnp.where(lane == 0, high, jnp.where(lane == 1, drop - high, 0.0))
        gx[h, :, 0:128] = scaled
        gx[h, :, 128:256] = extra.astype(BF16)

    def trade(i):
        at = pl.ds(i * 8, 8)
        return pltpu.make_async_remote_copy(
            terms.at[1 - c, at], r0.at[at], s0.at[i], t0.at[i], device_id=partner, device_id_type=MESH
        )

    half = iota((16, 128), 1) < 64

    def backward(i, dqs):
        rows = pl.ds(pl.multiple_of(i * CHUNK, CHUNK), CHUNK)
        new = []
        ropes = 0.0
        for h in range(2):
            p = pr[h, rows, :]
            diff = dot(vx[h, rows, :], gx[h], NT)
            ds = (p.astype(F32) * diff).astype(BF16)
            new.append(dqs[h] + dot(ds, kc[h, rows, :], TN))
            dk = dot(ds, qc[h]) * SCALE
            dd[:, 128 * h : 128 * (h + 1)] = dot(p, gx[h, :, 0:128]).astype(BF16)
            dd[:, 256 + 128 * h : 256 + 128 * (h + 1)] = dk[:, 0:128].astype(BF16)
            ropes = ropes + dk[:, 128:256]
        turned = pltpu.roll(ropes, 64, 1)
        tl = dot(dd[...], wkv[...]).astype(BF16)
        for q in range(16):
            chip = i * 8 + q // 2
            for l in range(4):
                terms[q % 2, chip, 32 * l : 32 * (l + 1), :] = tl[32 * q : 32 * (q + 1), 128 * l : 128 * (l + 1)]
            terms[q % 2, chip, 128:144, :] = jnp.where(
                half, ropes[32 * q : 32 * q + 16], turned[32 * q + 16 : 32 * q + 32]
            ).astype(BF16)
        trade(i).start()
        return tuple(new)

    dqs = lax.fori_loop(0, CHUNKS, backward, (nil, nil))
    for h in range(2):
        val = (dqs[h] * SCALE).astype(BF16)
        dq_out[:, 128 * h : 128 * (h + 1)] = val[:, 0:128]
        dp_out[:, 64 * h : 64 * (h + 1)] = val[:, 128:192]

    def add0(i, _):
        @pl.when(i % 8 == 0)
        def _():
            trade(i // 8).wait()

        at = (i // 16, (i // 4) % 4, i % 4)
        for k in range(3):
            o = ORDERS[k]
            rows = slice(48 * k, 48 * (k + 1))
            val = terms[c, i, rows, :].astype(F32) + r0[i, rows, :].astype(F32)
            a0[k, at[o[0]], at[o[1]], at[o[2]]] = val.astype(BF16)
        return 0

    lax.fori_loop(0, 64, add0, 0)

    def stage(i, src, dst):
        copies = []
        for o in range(1, 4):
            for k in range(3):
                d = ORDERS[k][i]
                copies.append(
                    pltpu.make_async_remote_copy(
                        src.at[k, (coord[d] + o) % 4], dst.at[k, o - 1],
                        ss.at[i, k, o - 1], rs.at[i, k, o - 1],
                        device_id=device(d, o), device_id_type=MESH,
                    )
                )
        for q in copies:
            q.start()
        for q in copies:
            q.wait()

    stage(0, a0, r1)
    for k in range(3):
        mine = coord[ORDERS[k][0]]

        def add1(i, _, k=k, mine=mine):
            val = a0[k, mine, i].astype(F32)
            for o in range(3):
                val = val + r1[k, o, i].astype(F32)
            a1[k, i] = val.astype(BF16)
            return 0

        lax.fori_loop(0, 4, add1, 0)
    stage(1, a1, r2)
    for k in range(3):
        val = a1[k, coord[ORDERS[k][1]]].astype(F32)
        for o in range(3):
            val = val + r2[k, o].astype(F32)
        a2[k] = val.astype(BF16)
    stage(2, a2, r3)
    for k in range(3):
        val = a2[k, coord[ORDERS[k][2]]].astype(F32)
        for o in range(3):
            val = val + r3[k, o].astype(F32)
        out[48 * k : 48 * (k + 1), :] = val


def attention(offs, back, comb, cot, keys, qn, qp, wkv, wout):
    vm = pl.BlockSpec(memory_space=pltpu.VMEM)
    sm = pl.BlockSpec(memory_space=pltpu.SMEM)
    dma = pltpu.SemaphoreType.DMA
    return pl.pallas_call(
        attention_kernel,
        out_shape=(
            jax.ShapeDtypeStruct((32, 2048), BF16),
            jax.ShapeDtypeStruct((256, 256), BF16),
            jax.ShapeDtypeStruct((256, 128), BF16),
            jax.ShapeDtypeStruct((144, 128), F32),
        ),
        in_specs=[sm, vm, vm, vm, vm, vm, vm, vm, vm],
        out_specs=(vm, vm, vm, vm),
        scratch_shapes=[
            pltpu.VMEM((64, 8, 1536), BF16),
            pltpu.VMEM((4, 2, 32, 2048), BF16),
            pltpu.VMEM((2, 4096, 256), BF16),
            pltpu.VMEM((2, 4096, 256), BF16),
            pltpu.VMEM((2, 4096, 256), F32),
            pltpu.VMEM((2, 4096, 256), BF16),
            pltpu.VMEM((2, 256, 256), BF16),
            pltpu.VMEM((2, 256, 256), BF16),
            pltpu.VMEM((CHUNK, 512), BF16),
            pltpu.VMEM((2, 64, 144, 128), BF16),
            pltpu.VMEM((64, 144, 128), BF16),
            pltpu.VMEM((3, 4, 4, 4, 48, 128), BF16),
            pltpu.VMEM((3, 3, 4, 4, 48, 128), BF16),
            pltpu.VMEM((3, 4, 4, 48, 128), BF16),
            pltpu.VMEM((3, 3, 4, 48, 128), BF16),
            pltpu.VMEM((3, 4, 48, 128), BF16),
            pltpu.VMEM((3, 3, 48, 128), BF16),
            dma((64,)), dma((64,)), dma, dma((4,)), dma((4,)),
            dma((CHUNKS,)), dma((CHUNKS,)), dma((3, 3, 3)), dma((3, 3, 3)),
        ],
        compiler_params=pltpu.CompilerParams(
            collective_id=1, has_side_effects=True, vmem_limit_bytes=62 * 1024 * 1024
        ),
        cost_estimate=pl.CostEstimate(flops=11 * 10**9, bytes_accessed=10 * 10**6, transcendentals=2 * 10**6),
    )(offs, back, comb, cot, keys, qn, qp, wkv, wout)


def on_device(
    hidden, cotangent, routes, gates, offsets, w_gate, w_up, w_down, w_out,
    latent, rope_key, q_nope, q_pe, w_uk, w_uv,
):
    blank = jnp.zeros_like(rope_key)
    keys = lax.all_gather(
        jnp.concatenate([latent, rope_key, blank], axis=1), "wide", axis=0, tiled=True
    )
    back, comb = experts(
        routes.T, gates.T, hidden, cotangent, w_gate[0].T, w_up[0].T, w_down[0]
    )
    resid_grad, dq, dpe, mine = attention(
        offsets, back, comb, cotangent, keys, q_nope, q_pe,
        jnp.concatenate([w_uv, w_uk], axis=0), w_out,
    )
    grad_latent = mine[:128].reshape(4, 32, 128).transpose(1, 0, 2).reshape(32, 512)
    grad_rope = mine[128:].reshape(16, 2, 64).transpose(1, 0, 2).reshape(32, 64)
    return (resid_grad, dq, dpe, grad_latent, grad_rope)


def solution(mesh):
    both = ("wide", "narrow")
    return jax.shard_map(
        on_device,
        mesh=mesh,
        in_specs=(
            P(both, None), P(both, None), P(both, None), P(both, None), P(),
            P(both, None, None), P(both, None, None), P(both, None, None),
            P("narrow", None), P("wide", None), P("wide", None),
            P("wide", "narrow"), P("wide", "narrow"), P("narrow", None), P("narrow", None),
        ),
        out_specs=(
            P(both, None), P("wide", "narrow"), P("wide", "narrow"), P(both, None), P(both, None),
        ),
        check_vma=False,
    )
```

profile of v0, /device:TPU:0, one launch (start us, length us, event | category | flops | bytes accessed | tf_op | source)
XLA Modules:
  0.0 186.8 jit_solution(7397668404270727302)
XLA Ops:
  7.2 0.0 all-gather.2.cloned.1.call-start
  7.2 0.9 copy.20
  8.1 0.1 pad.4.clone
  8.2 1.7 maximum_maximum_fusion
  9.9 0.0 all-gather.2.cloned.1.call-update
  9.9 1.8 pad_maximum_fusion.wkv
  11.8 72.0 %shard_map.182 = (bf16[64,8,1536]{2,1,0:T(8,128)(2,1)}, bf16[4,512,32]{2,1,0:T(8,128)(2,1)}) custom-call(s32[6,32]{1,0:T(8,128)} %bitcast.25, f32[6,32]{1,0:T(8,128)} %bitcast.26, bf16[32,2048]{1,0:T(8,128)(2,1)} %hid.1, bf16[32,2048]{1,0:T(8,128)(2,1)} %cot.3, bf16[704,2048]{1,0:T(8,128)(2,1)} %bitcast.22, bf16[704,2048]{1,0:T(8,128)(2,1)} %bitcast.23, ...), custom_call_target="tpu_custom_call" | custom-call | flops 11000000512 | bytes 20000000 | tf_op jit(solution)/shard_map/pallas_call | solution.py:210
  83.8 8.2 %all-gather.2.cloned.1.call-done.keys = bf16[4096,640]{1,0:T(8,128)(2,1)} async-done(((bf16[256,640]{1,0:T(8,128)(2,1)}), bf16[4096,640]{1,0:T(8,128)(2,1)}) %all-gather.2.cloned.1.call-update) | async-done | bytes 5242896 | tf_op jit(solution)/shard_map/all_gather | solution.py:532
  91.9 80.5 %shard_map.183 = (bf16[32,2048]{1,0:T(8,128)(2,1)}, bf16[256,256]{1,0:T(8,128)(2,1)}, bf16[256,128]{1,0:T(8,128)(2,1)}, f32[144,128]{1,0:T(8,128)}) custom-call(s32[16]{0:T(128)} %offs.1, bf16[64,8,1536]{2,1,0:T(8,128)(2,1)} %get-tuple-element.11.back, bf16[4,512,32]{2,1,0:T(8,128)(2,1)} %get-tuple-element.12.comb, bf16[32,2048]{1,0:T(8,128)(2,1)} %cot.3, ...), custom_call_target="tpu_custom_call" | custom-call | flops 11000000512 | bytes 10000000 | tf_op jit(solution)/shard_map/pallas_call | solution.py:489
  172.5 0.7 slice.7
  173.2 0.8 slice.6
  174.0 0.6 copy.25
  174.6 0.1 reshape.24
  174.7 0.6 copy.22
  175.3 1.6 copy.29
  176.9 1.6 copy.30
  178.5 1.5 copy.31
  (1 shorter events, 0.0 us)
Async XLA Ops:
  7.2 84.7 %all-gather.2.cloned.1.call-start = ((), (), s32[]{:S(2)}) async-start(), calls=%async_computation | async-start | bytes 5570560 | tf_op jit(solution)/shard_map/all_gather | solution.py:532
Sparse Core Ops, SparseCore 0:
  10.1 81.7 all-gather.1
where the time goes:
time: 187 us
  Pallas kernels  152 us (81%)
  between operations  14.1 us (8%)
  local copies, waits for them, and re-layouts  8.42 us (5%)
  waiting for transfers between devices  8.18 us (4%)
  other arithmetic  3.58 us (2%)
    pallas_call x1, Pallas kernels, attention(): pl.pallas_call(attention_kernel, out_shape=(jax.ShapeDtypeStruct((32, 204...  80.5 us
    pallas_call x1, Pallas kernels, experts(): pl.pallas_call(experts_kernel, out_shape=(jax.ShapeDtypeStruct((64, 8, 15...  72 us
    all_gather x1, waiting for transfers between devices, on_device(): lax.all_gather(jnp.concatenate([latent, rope_key, blank], axis=1), 'wide'...  8.16 us
    unnamed x4, local copies, waits for them, and re-layouts  5.48 us
  transfers between devices with their start and end apart: 1, of which 1 were waited for; matrix products, arithmetic and copies ran while one was open for 1% of the time, Pallas kernels for 39%

commit v1 on v0

v1 whole, which is shorter than its diff:
```python
import functools
import math

import jax
import jax.numpy as jnp
from jax import lax
from jax.experimental import pallas as pl
from jax.experimental.pallas import tpu as pltpu
from jax.sharding import PartitionSpec as P

LATENT = 512
NOPE = 128
ROPE = 64
VDIM = 128
MESH = pl.DeviceIdType.MESH
F32 = jnp.float32
BF16 = jnp.bfloat16
NT = (((1,), (1,)), ((), ()))
NN = (((1,), (0,)), ((), ()))
TN = (((0,), (0,)), ((), ()))


def dot(a, b, dims=NN):
    return lax.dot_general(a, b, dims, preferred_element_type=F32)


def iota(shape, dim):
    return lax.broadcasted_iota(jnp.int32, shape, dim)


def place():
    w = lax.axis_index("wide")
    n = lax.axis_index("narrow")
    return w // 4, w % 4, n // 2, n % 2


def selections(rt, gt):
    expert = iota((512, 32), 0) >> 3
    named = jnp.zeros((512, 32), F32)
    weight = jnp.zeros((512, 32), F32)
    for k in range(6):
        hit = expert == rt[k : k + 1, :]
        named = jnp.where(hit, 1.0, named)
        weight = jnp.where(hit, gt[k : k + 1, :], weight)
    earlier = (iota((32, 32), 0) < iota((32, 32), 1)).astype(F32).astype(BF16)
    before = dot(named.astype(BF16), earlier)
    row = iota((512, 32), 0) & 7
    picks = []
    for j in range(3):
        slot = jnp.where(row < 6, row, jnp.where(row == 6, j, 3 + j))
        picks.append(jnp.where(before == slot.astype(F32), named, 0.0))
    return picks, weight, row


def pack_matrix(j):
    q = iota((192, 256), 1)
    r = iota((192, 256), 0)
    s = q & 7
    base = (q >> 3) * 6
    if j < 0:
        return ((s < 6) & (r == base + s)).astype(F32).astype(BF16)
    return ((s >= 6) & (r == base + (s - 6) * 3 + j)).astype(F32).astype(BF16)


def fold_matrix(j):
    q = iota((256, 192), 0)
    r = iota((256, 192), 1)
    s = q & 7
    base = (q >> 3) * 6
    if j < 0:
        return ((s < 6) & (r == base + s)).astype(F32).astype(BF16)
    return ((s >= 6) & (r == base + (s - 6) * 3 + j)).astype(F32).astype(BF16)


ORDERS = ((2, 0, 1), (0, 1, 2), (1, 2, 0))
CHUNK = 512
CHUNKS = 8
SCALE = 1.0 / math.sqrt(NOPE + ROPE)


def layer_kernel(
    offs, rt, gt, hid, cot, lat, rope, qn, qp, wuv, wuk, wout, wg, wu, wd,
    own_out, dq_out, dp_out, out,
    send, recv, wgb, wub, wdb, back, landed, keys, gathered, comb, xs, dys, sc,
    wkv, qc, gx, dd, terms, r0, r1, ry, a1, r2, a2, r3,
    lsem, psem, ssem, rsem, wssem, wrsem, bssem, brsem, asem, bsem, gsem, hsem,
    s0, t0, s1, t1, sy, ty, ss, rs,
):
    y, x, z, c = place()
    coord = (y, x, z)
    me = (y * 4 + x) * 4 + z
    partner = (y * 4 + x, z * 2 + 1 - c)

    def peer(k, sign=1):
        k = (k * 11) % 64
        pw = ((y + 4 + sign * (k // 16)) % 4) * 4 + (x + 4 + sign * ((k // 4) % 4)) % 4
        pz = (z + 4 + sign * (k % 4)) % 4
        return pw * 4 + pz, (pw, pz * 2 + c)

    def device(d, o):
        at = list(coord)
        at[d] = (at[d] + o) % 4
        return (at[0] * 4 + at[1], at[2] * 2 + c)

    def remote(src, dst, a, b, dev):
        return pltpu.make_async_remote_copy(
            src_ref=src, dst_ref=dst, send_sem=a, recv_sem=b, device_id=dev, device_id_type=MESH
        )

    bar = pltpu.get_barrier_semaphore()

    def greet(k, _):
        pl.semaphore_signal(bar, inc=1, device_id=peer(k)[1], device_id_type=MESH)
        return 0

    lax.fori_loop(1, 64, greet, 0)
    pl.semaphore_signal(bar, inc=1, device_id=partner, device_id_type=MESH)
    weights = ((wg, wgb), (wu, wub), (wd, wdb))
    loads = [pltpu.make_async_copy(a, b.at[0], lsem.at[i]) for i, (a, b) in enumerate(weights)]
    for q in loads:
        q.start()

    picks, weight, row = selections(rt[...], gt[...])
    cot_hi = cot[:, 1024:2048]
    for j in range(3):
        low = jnp.where(row < 6, picks[j], 0.0).astype(BF16)
        high = jnp.where(row < 6, 0.0, picks[j]).astype(BF16)
        if j == 0:
            comb[0] = low
        comb[1 + j] = high
        part = (hid[:, 0:1024], hid[:, 1024:2048], cot[:, 0:1024])[j]
        gate = jnp.sum(picks[j] * weight, axis=1, keepdims=True)
        if j < 2:
            gate = jnp.where(row[:, 0:1] < 6, 1.0, gate)
        val = (dot(low, part) + dot(high, cot_hi)) * gate
        send[:, :, 1024 * j : 1024 * (j + 1)] = val.astype(BF16).reshape(64, 8, 1024)
    zero = jnp.zeros((256, 64), BF16)
    keys[y, x, :, :, :, 0:512] = lat[...].reshape(2, 2, 64, 512)
    keys[y, x, :, :, :, 512:640] = jnp.concatenate([rope[...], zero], axis=1).reshape(2, 2, 64, 128)

    pl.semaphore_wait(bar, 64)

    def start(k, _):
        pc, dev = peer(k)
        remote(send.at[pc], recv.at[k], ssem.at[k], rsem.at[k], dev).start()
        return 0

    trades = [
        remote(a, b.at[1], wssem.at[i], wrsem.at[i], partner) for i, (a, b) in enumerate(weights)
    ]
    spread = []
    for k, d in ((0, 1), (1, 0)):
        for o in range(1, 4):
            at = keys.at[y, x, c, k]
            spread.append(remote(at, at, asem.at[0, k, o - 1], bsem.at[0, k, o - 1], device(d, o)))
    own = pltpu.make_async_copy(send.at[me], recv.at[0], psem)
    own.start()
    lax.fori_loop(1, 64, start, 0)
    for q in trades:
        q.start()
    for q in spread:
        q.start()
    for h in range(2):
        qc[h, :, 0:128] = qn[:, 128 * h : 128 * (h + 1)]
        qc[h, :, 128:256] = jnp.concatenate([qp[:, 64 * h : 64 * (h + 1)], zero], axis=1)
    wkv[0:256, :] = wuv[...]
    wkv[256:512, :] = wuk[...]
    own.wait()

    def arrive(k, _):
        remote(send.at[0], recv.at[k], ssem.at[k], rsem.at[k], partner).wait_recv()
        return 0

    def ret_start(k, _):
        remote(back.at[k], landed.at[me], bssem.at[k], brsem.at[me], peer(k, -1)[1]).start()
        return 0

    widen = []
    for k, d in ((0, 0), (1, 1)):
        for o in range(1, 4):
            at = keys.at[y, :, c, 0] if k == 0 else keys.at[:, x, c, 1]
            widen.append(remote(at, at, asem.at[1, k, o - 1], bsem.at[1, k, o - 1], device(d, o)))
    mirror = remote(keys.at[:, :, c], keys.at[:, :, c], gsem.at[4], hsem.at[4], partner)

    for g in range(2):
        lax.fori_loop(max(1, 32 * g), 32 * (g + 1), arrive, 0)
        plain = pack_matrix(-1)

        def cols(a, b, g=g):
            return recv[32 * g : 32 * (g + 1), :, a:b].reshape(256, b - a)

        xs[:, 0:1024] = dot(plain, cols(0, 1024)).astype(BF16)
        xs[:, 1024:2048] = dot(plain, cols(1024, 2048)).astype(BF16)
        dys[:, 0:1024] = dot(plain, cols(2048, 3072)).astype(BF16)
        hi = dot(pack_matrix(0), cols(0, 1024))
        hi = hi + dot(pack_matrix(1), cols(1024, 2048))
        hi = hi + dot(pack_matrix(2), cols(2048, 3072))
        dys[:, 1024:2048] = hi.astype(BF16)
        if g == 0:
            for q in loads:
                q.wait()
        for h in range(2):
            if g == 0 and h == 1:
                for q in trades:
                    q.wait()
            if g == 1 and h == 1:
                for q in widen:
                    q.wait()
                mirror.start()
            pre = dot(xs[...], wgb[h], NT)
            up = dot(xs[...], wub[h], NT)
            gh = dot(dys[...], wdb[h], NT)
            s = jax.nn.sigmoid(pre)
            gg = (gh * up * s * (1.0 + pre * (1.0 - s))).astype(BF16)
            gu = (gh * pre * s).astype(BF16)
            for b in range(2):
                cs = slice(1024 * b, 1024 * (b + 1))
                term = dot(gg, wgb[h, :, cs]) + dot(gu, wub[h, :, cs])
                if h == 0:
                    sc[0, 0:192, cs] = term
                else:
                    xs[:, cs] = (sc[0, 0:192, cs] + term).astype(BF16)
        plain = fold_matrix(-1)
        for j in range(3):
            val = dot(plain, xs[:, 512 * j : 512 * (j + 1)])
            val = val + dot(fold_matrix(j), xs[:, 1536:2048])
            back[32 * g : 32 * (g + 1), :, 512 * j : 512 * (j + 1)] = val.astype(BF16).reshape(32, 8, 512)
        if g == 0:
            for q in spread:
                q.wait()
            for q in widen:
                q.start()
            own = pltpu.make_async_copy(back.at[0], landed.at[me], psem)
            own.start()
        lax.fori_loop(max(1, 32 * g), 32 * (g + 1), ret_start, 0)

    mirror.wait()
    ones = (iota((CHUNK, 128), 1) < 2).astype(F32).astype(BF16)
    delta = iota((256, 256), 0) - iota((256, 256), 1)
    here = offs[y * 4 + x]

    def block(i):
        return slice(0, CHUNK), pl.ds(pl.multiple_of(i * 256, 256), 256)

    def forward(i, tops):
        sub, at = block(i)
        chunk = keys[i // 2, pl.ds((i % 2) * 2, 2)].reshape(CHUNK, 640)
        kv = dot(chunk[:, 0:512], wkv[...], NT).astype(BF16)
        new = []
        for h in range(2):
            vx = jnp.concatenate([kv[:, 128 * h : 128 * (h + 1)], ones], axis=1)
            kc = jnp.concatenate([kv[:, 256 + 128 * h : 256 + 128 * (h + 1)], chunk[:, 512:640]], axis=1)
            wdb[h, sub, at] = vx
            wub[h, sub, at] = kc
            top = tops[h]
            val = dot(kc, qc[h], NT)
            for b in range(2):
                limit = (here - offs[2 * i + b]) * 256
                part = jnp.where(delta <= limit, val[256 * b : 256 * (b + 1)], -1e30)
                sc[h, 256 * b : 256 * (b + 1), at] = part
                top = jnp.maximum(top, jnp.max(part.reshape(32, 8, 256), axis=0))
            new.append(top)
        return tuple(new)

    least = jnp.full((8, 256), -1e30, F32)
    tops = lax.fori_loop(0, CHUNKS, forward, (least, least))
    tops = [jnp.max(t, axis=0, keepdims=True) for t in tops]

    def weigh(i, sums):
        sub, at = block(i)
        new = []
        for h in range(2):
            p = jnp.exp(SCALE * (sc[h, sub, at] - tops[h])).astype(BF16)
            wgb[h, sub, at] = p
            new.append(sums[h] + dot(p, wdb[h, sub, at], TN))
        return tuple(new)

    nil = jnp.zeros((256, 256), F32)
    sums = lax.fori_loop(0, CHUNKS, weigh, (nil, nil))

    own.wait()

    def ret_finish(k, _):
        pc = peer(k)[0]
        remote(send.at[0], recv.at[k], ssem.at[k], rsem.at[k], partner).wait_send()
        q = remote(back.at[k], landed.at[pc], bssem.at[k], brsem.at[pc], partner)
        q.wait_send()
        q.wait_recv()
        return 0

    lax.fori_loop(1, 64, ret_finish, 0)

    total = cot[...].astype(F32)
    rest = jnp.zeros((32, 512), F32)
    for j in range(3):
        part = landed[:, :, 512 * j : 512 * (j + 1)].reshape(512, 512)
        cs = slice(512 * j, 512 * (j + 1))
        own_out[:, cs] = (total[:, cs] + dot(comb[0], part, TN)).astype(BF16)
        rest = rest + dot(comb[1 + j], part, TN)
    own_out[:, 1536:2048] = (total[:, 1536:2048] + rest).astype(BF16)
    gathered[z, c] = own_out[...]
    hops = [
        remote(own_out, gathered.at[z, c], gsem.at[o - 1], hsem.at[o - 1], device(2, o))
        for o in range(1, 4)
    ]
    for q in hops:
        q.start()
    for q in hops:
        q.wait()
    last = remote(gathered.at[:, c], gathered.at[:, c], gsem.at[3], hsem.at[3], partner)
    last.start()
    last.wait()

    go = dot(gathered[...].reshape(256, 2048), wout[...], NT).astype(BF16).astype(F32)
    lane = iota((256, 128), 1)
    for h in range(2):
        inv = 1.0 / sums[h][:, 128:129]
        mean = sums[h][:, 0:128] * inv
        scaled = (go[:, 128 * h : 128 * (h + 1)] * inv).astype(BF16)
        drop = -jnp.sum(scaled.astype(F32) * mean, axis=1, keepdims=True)
        high = drop.astype(BF16).astype(F32)
        extra = jnp.where(lane == 0, high, jnp.where(lane == 1, drop - high, 0.0))
        gx[h, :, 0:128] = scaled
        gx[h, :, 128:256] = extra.astype(BF16)

    def trade(r):
        g = (y + 1 + r) % 4
        return remote(terms.at[1 - c, g], r0.at[g], s0.at[r], t0.at[r], partner)

    left = iota((16, 128), 1) < 64

    def backward(i, dqs):
        sub, at = block(i)
        new = []
        ropes = 0.0
        for h in range(2):
            p = wgb[h, sub, at]
            diff = dot(wdb[h, sub, at], gx[h], NT)
            ds = (p.astype(F32) * diff).astype(BF16)
            new.append(dqs[h] + dot(ds, wub[h, sub, at], TN))
            dk = dot(ds, qc[h]) * SCALE
            dd[:, 128 * h : 128 * (h + 1)] = dot(p, gx[h, :, 0:128]).astype(BF16)
            dd[:, 256 + 128 * h : 256 + 128 * (h + 1)] = dk[:, 0:128].astype(BF16)
            ropes = ropes + dk[:, 128:256]
        turned = pltpu.roll(ropes, 64, 1)
        tl = dot(dd[...], wkv[...]).astype(BF16)
        for q in range(16):
            e, f, m = i // 2, (i % 2) * 2 + q // 8, (q // 2) % 4
            for l in range(4):
                terms[q % 2, e, f, m, 32 * l : 32 * (l + 1), :] = tl[32 * q : 32 * (q + 1), 128 * l : 128 * (l + 1)]
            terms[q % 2, e, f, m, 128:144, :] = jnp.where(
                left, ropes[32 * q : 32 * q + 16], turned[32 * q + 16 : 32 * q + 32]
            ).astype(BF16)
        return tuple(new)

    def near(r, k, o):
        g = (y + 1 + r) % 4
        d = ORDERS[k][0]
        rows = pl.ds(48 * k, 48)
        to = (coord[d] + o) % 4
        src = terms.at[c, g, :, to, rows] if k == 0 else terms.at[c, g, to, :, rows]
        i = k // 2
        return remote(src, r1.at[i, o - 1, g], s1.at[i, o - 1, r], t1.at[i, o - 1, r], device(d, o))

    def far(r):
        g = (y + 1 + r) % 4
        pz = z * 2 + c
        return remote(terms.at[c, g, :, :, pl.ds(48, 48)], ry.at[r], sy.at[r], ty.at[r], (g * 4 + x, pz))

    def settle(r):
        trade(r).wait()
        g = (y + 1 + r) % 4

        def add(i, _):
            a, b = i // 4, i % 4
            val = terms[c, g, a, b].astype(F32) + r0[g, a, b].astype(F32)
            terms[c, g, a, b] = val.astype(BF16)
            return 0

        lax.fori_loop(0, 16, add, 0)
        for o in range(1, 4):
            near(r, 0, o).start()
            near(r, 2, o).start()

        @pl.when(r < 3)
        def _():
            far(r).start()

    def quarter(r, dqs):
        i = ((y + 1 + r) % 4) * 2
        dqs = lax.fori_loop(i, i + 2, backward, dqs)
        trade(r).start()

        @pl.when(r > 0)
        def _():
            settle(r - 1)

        return dqs

    dqs = lax.fori_loop(0, 4, quarter, (nil, nil))
    for h in range(2):
        val = (dqs[h] * SCALE).astype(BF16)
        dq_out[:, 128 * h : 128 * (h + 1)] = val[:, 0:128]
        dp_out[:, 64 * h : 64 * (h + 1)] = val[:, 128:192]
    settle(3)

    def close(r, _):
        for o in range(1, 4):
            near(r, 0, o).wait()
            near(r, 2, o).wait()

        @pl.when(r < 3)
        def _():
            far(r).wait()

        return 0

    lax.fori_loop(0, 4, close, 0)

    def add1(i, _):
        a, b = i // 4, i % 4
        val = terms[c, a, b, z, 0:48].astype(F32)
        for o in range(3):
            val = val + r1[0, o, a, b].astype(F32)
        a1[0, a, b] = val.astype(BF16)
        val = terms[c, y, a, b, 48:96].astype(F32)
        for o in range(3):
            val = val + ry[o, a, b].astype(F32)
        a1[1, a, b] = val.astype(BF16)
        val = terms[c, a, x, b, 96:144].astype(F32)
        for o in range(3):
            val = val + r1[1, o, a, b].astype(F32)
        a1[2, b, a] = val.astype(BF16)
        return 0

    lax.fori_loop(0, 16, add1, 0)

    def stage(i, src, dst):
        copies = []
        for o in range(1, 4):
            for k in range(3):
                d = ORDERS[k][i]
                copies.append(
                    remote(
                        src.at[k, (coord[d] + o) % 4], dst.at[k, o - 1],
                        ss.at[i - 1, k, o - 1], rs.at[i - 1, k, o - 1], device(d, o),
                    )
                )
        for q in copies:
            q.start()
        for q in copies:
            q.wait()

    stage(1, a1, r2)
    for k in range(3):
        val = a1[k, coord[ORDERS[k][1]]].astype(F32)
        for o in range(3):
            val = val + r2[k, o].astype(F32)
        a2[k] = val.astype(BF16)
    stage(2, a2, r3)
    for k in range(3):
        val = a2[k, coord[ORDERS[k][2]]].astype(F32)
        for o in range(3):
            val = val + r3[k, o].astype(F32)
        out[48 * k : 48 * (k + 1), :] = val


def layer(*args):
    vm = pl.BlockSpec(memory_space=pltpu.VMEM)
    sm = pl.BlockSpec(memory_space=pltpu.SMEM)
    hbm = pl.BlockSpec(memory_space=pl.ANY)
    dma = pltpu.SemaphoreType.DMA
    half = args[-1].shape[0]

    def room(*shape, dtype=BF16):
        return pltpu.VMEM(shape, dtype)

    return pl.pallas_call(
        layer_kernel,
        out_shape=(
            jax.ShapeDtypeStruct((32, 2048), BF16),
            jax.ShapeDtypeStruct((256, 256), BF16),
            jax.ShapeDtypeStruct((256, 128), BF16),
            jax.ShapeDtypeStruct((144, 128), F32),
        ),
        in_specs=[sm] + [vm] * 11 + [hbm] * 3,
        out_specs=(vm, vm, vm, vm),
        scratch_shapes=[
            room(64, 8, 3072), room(64, 8, 3072),
            room(2, half, 2048), room(2, half, 2048), room(2, half, 2048),
            room(64, 8, 1536), room(64, 8, 1536),
            room(4, 4, 2, 2, 64, 640), room(4, 2, 32, 2048), room(4, 512, 32),
            room(192, 2048), room(192, 2048), room(2, 512, 2048, dtype=F32),
            room(512, 512), room(2, 256, 256), room(2, 256, 256), room(CHUNK, 512),
            room(2, 4, 4, 4, 144, 128), room(4, 4, 4, 144, 128),
            room(2, 3, 4, 4, 48, 128), room(3, 4, 4, 48, 128),
            room(3, 4, 4, 48, 128), room(3, 3, 4, 48, 128),
            room(3, 4, 48, 128), room(3, 3, 48, 128),
            dma((3,)), dma, dma((64,)), dma((64,)), dma((3,)), dma((3,)),
            dma((64,)), dma((64,)), dma((2, 2, 3)), dma((2, 2, 3)), dma((5,)), dma((5,)),
            dma((4,)), dma((4,)), dma((2, 3, 4)), dma((2, 3, 4)), dma((3,)), dma((3,)),
            dma((2, 3, 3)), dma((2, 3, 3)),
        ],
        compiler_params=pltpu.CompilerParams(
            collective_id=0, has_side_effects=True, vmem_limit_bytes=67043328
        ),
        cost_estimate=pl.CostEstimate(flops=22 * 10**9, bytes_accessed=20 * 10**6, transcendentals=3 * 10**6),
    )(*args)


def on_device(
    hidden, cotangent, routes, gates, offsets, w_gate, w_up, w_down, w_out,
    latent, rope_key, q_nope, q_pe, w_uk, w_uv,
):
    resid_grad, dq, dpe, mine = layer(
        offsets, routes.T, gates.T, hidden, cotangent, latent, rope_key, q_nope, q_pe,
        w_uv, w_uk, w_out, w_gate[0].T, w_up[0].T, w_down[0],
    )
    grad_latent = mine[:128].reshape(4, 32, 128).transpose(1, 0, 2).reshape(32, 512)
    grad_rope = mine[128:].reshape(16, 2, 64).transpose(1, 0, 2).reshape(32, 64)
    return (resid_grad, dq, dpe, grad_latent, grad_rope)


def solution(mesh):
    both = ("wide", "narrow")
    return jax.shard_map(
        on_device,
        mesh=mesh,
        in_specs=(
            P(both, None), P(both, None), P(both, None), P(both, None), P(),
            P(both, None, None), P(both, None, None), P(both, None, None),
            P("narrow", None), P("wide", None), P("wide", None),
            P("wide", "narrow"), P("wide", "narrow"), P("narrow", None), P("narrow", None),
        ),
        out_specs=(
            P(both, None), P("wide", "narrow"), P("wide", "narrow"), P(both, None), P(both, None),
        ),
        check_vma=False,
    )
```

time: 187 us -> 145 us (0.78)
  Pallas kernels: 152 us -> 135 us
  between operations: 14.1 us -> 0.64 us
  waiting for transfers between devices: 8.18 us -> 0 us
  other arithmetic: 3.58 us -> 0 us
    pallas_call x2 -> x1, Pallas kernels: 152 us -> 135 us  [layer(): pl.pallas_call(layer_kernel, out_shape=(jax.ShapeDtypeStruct((32, 2048),...]
    all_gather x1 -> x0, waiting for transfers between devices: 8.16 us -> none  [on_device(): lax.all_gather(jnp.concatenate([latent, rope_key, blank], axis=1), 'wide'...]
    concatenate x2 -> x0, other arithmetic: 3.58 us -> none  [the longest x1 1.84 us: on_device(): jnp.concatenate([w_uv, w_uk], axis=0)]
  transfers between devices with their start and end apart: 1 -> 0, of which waited for: 1 -> 0; matrix products, arithmetic and copies ran while one was open for 1% -> 0% of each run, Pallas kernels for 39% -> 0%
where the time goes in v1:
time: 145 us; the launch traced here: 144 us
  Pallas kernels  135 us (93%)
  local copies, waits for them, and re-layouts  8.97 us (6%)
    pallas_call x1, Pallas kernels, layer(): pl.pallas_call(layer_kernel, out_shape=(jax.ShapeDtypeStruct((32, 2048),...  135 us
    unnamed x4, local copies, waits for them, and re-layouts  6.1 us

profile of v1, /device:TPU:0, one launch (start us, length us, event | category | flops | bytes accessed | tf_op | source)
XLA Modules:
  0.0 144.3 jit_solution(12748202411000717433)
XLA Ops:
  0.6 1.5 %copy.20.rope = bf16[256,64]{1,0:T(8,128)(2,1)} copy(bf16[256,64]{0,1:T(8,128)(2,1)} %param.25) | data formatting | bytes 65536 | tf_op args[10]
  2.1 134.6 %shard_map.182 = (bf16[32,2048]{1,0:T(8,128)(2,1)}, bf16[256,256]{1,0:T(8,128)(2,1)}, bf16[256,128]{1,0:T(8,128)(2,1)}, f32[144,128]{1,0:T(8,128)}) custom-call(s32[16]{0:T(128)} %offs.1, s32[6,32]{1,0:T(8,128)} %bitcast.25, f32[6,32]{1,0:T(8,128)} %bitcast.26, bf16[32,2048]{1,0:T(8,128)(2,1)} %hid.1, bf16[32,2048]{1,0:T(8,128)(2,1)} %cot.1, ...), custom_call_target="tpu_custom_call" | custom-call | flops 22000001024 | bytes 20000000 | tf_op jit(solution)/shard_map/pallas_call | solution.py:478
  136.8 0.8 slice.6
  137.6 0.6 copy.25
  138.3 0.7 slice.7
  139.0 0.1 reshape.24
  139.0 0.6 copy.22
  139.6 1.6 %copy.29 = bf16[32,2048]{1,0:T(8,128)(2,1)} copy(bf16[32,2048]{1,0:T(8,128)(2,1)} %get-tuple-element.18) | data formatting | bytes 262144
  141.2 1.6 %copy.30 = bf16[256,256]{1,0:T(8,128)(2,1)} copy(bf16[256,256]{1,0:T(8,128)(2,1)} %get-tuple-element.19) | data formatting | bytes 262144
  142.8 1.5 %copy.31 = bf16[256,128]{1,0:T(8,128)(2,1)} copy(bf16[256,128]{1,0:T(8,128)(2,1)} %get-tuple-element.20) | data formatting | bytes 131072

commit v2 on v1

--- a/solution.py
+++ b/solution.py
@@ -79,11 +79,12 @@
 
 
 def layer_kernel(
-    offs, rt, gt, hid, cot, lat, rope, qn, qp, wuv, wuk, wout, wg, wu, wd,
-    own_out, dq_out, dp_out, out,
+    offs, rt_h, gt_h, hid_h, cot_h, lat_h, rope_h, qn_h, qp_h, wuv_h, wuk_h, wout_h, wg, wu, wd,
+    own_h, dq_h, dp_h, out,
+    rt, gt, hid, cot, rope, qn, qp, wout, own_out, dq_out, dp_out,
     send, recv, wgb, wub, wdb, back, landed, keys, gathered, comb, xs, dys, sc,
     wkv, qc, gx, dd, terms, r0, r1, ry, a1, r2, a2, r3,
-    lsem, psem, ssem, rsem, wssem, wrsem, bssem, brsem, asem, bsem, gsem, hsem,
+    fsem, osem, sync, lsem, psem, ssem, rsem, wssem, wrsem, bssem, brsem, asem, bsem, gsem, hsem,
     s0, t0, s1, t1, sy, ty, ss, rs,
 ):
     y, x, z, c = place()
@@ -109,20 +110,52 @@
 
     bar = pltpu.get_barrier_semaphore()
 
-    def greet(k, _):
-        pl.semaphore_signal(bar, inc=1, device_id=peer(k)[1], device_id_type=MESH)
-        return 0
-
-    lax.fori_loop(1, 64, greet, 0)
     pl.semaphore_signal(bar, inc=1, device_id=partner, device_id_type=MESH)
+    for d in range(3):
+        for o in range(1, 4):
+            pl.semaphore_signal(bar, inc=1, device_id=device(d, o), device_id_type=MESH)
+    fetches = [
+        (rt_h, rt), (gt_h, gt), (hid_h, hid), (cot_h, cot), (rope_h, rope),
+        (lat_h.at[pl.ds(128 * c, 64)], keys.at[y, x, c, 0, :, pl.ds(0, 512)]),
+        (lat_h.at[pl.ds(128 * c + 64, 64)], keys.at[y, x, c, 1, :, pl.ds(0, 512)]),
+        (qn_h, qn), (qp_h, qp), (wuv_h, wkv.at[pl.ds(0, 256)]), (wuk_h, wkv.at[pl.ds(256, 256)]),
+        (wout_h, wout),
+    ]
+    fetches = [pltpu.make_async_copy(a, b, fsem.at[i]) for i, (a, b) in enumerate(fetches)]
+    for q in fetches:
+        q.start()
     weights = ((wg, wgb), (wu, wub), (wd, wdb))
     loads = [pltpu.make_async_copy(a, b.at[0], lsem.at[i]) for i, (a, b) in enumerate(weights)]
     for q in loads:
         q.start()
+    for q in fetches[:7]:
+        q.wait()
+    eye = (iota((64, 128), 0) == iota((64, 128), 1)).astype(F32).astype(BF16)
+    turned = dot(rope[...], eye, TN).astype(BF16).reshape(2, 2, 64, 128)
+    for h in range(2):
+
+        @pl.when(c == h)
+        def _(h=h):
+            keys[y, x, h, :, :, 512:640] = turned[h]
+
+    pl.semaphore_wait(bar, 10)
+    spread = []
+    for k, d in ((0, 1), (1, 0)):
+        for o in range(1, 4):
+            at = keys.at[y, x, c, k]
+            spread.append(remote(at, at, asem.at[0, k, o - 1], bsem.at[0, k, o - 1], device(d, o)))
+    for q in spread:
+        q.start()
+    for o in range(1, 4):
+        pl.semaphore_signal(sync.at[0], inc=1, device_id=device(0, o), device_id_type=MESH)
 
     picks, weight, row = selections(rt[...], gt[...])
     cot_hi = cot[:, 1024:2048]
     for j in range(3):
+        if j == 1:
+            pl.semaphore_wait(sync.at[0], 3)
+            for o in range(1, 4):
+                pl.semaphore_signal(sync.at[1], inc=1, device_id=device(2, o), device_id_type=MESH)
         low = jnp.where(row < 6, picks[j], 0.0).astype(BF16)
         high = jnp.where(row < 6, 0.0, picks[j]).astype(BF16)
         if j == 0:
@@ -135,10 +168,7 @@
         val = (dot(low, part) + dot(high, cot_hi)) * gate
         send[:, :, 1024 * j : 1024 * (j + 1)] = val.astype(BF16).reshape(64, 8, 1024)
     zero = jnp.zeros((256, 64), BF16)
-    keys[y, x, :, :, :, 0:512] = lat[...].reshape(2, 2, 64, 512)
-    keys[y, x, :, :, :, 512:640] = jnp.concatenate([rope[...], zero], axis=1).reshape(2, 2, 64, 128)
-
-    pl.semaphore_wait(bar, 64)
+    pl.semaphore_wait(sync.at[1], 3)
 
     def start(k, _):
         pc, dev = peer(k)
@@ -148,23 +178,16 @@
     trades = [
         remote(a, b.at[1], wssem.at[i], wrsem.at[i], partner) for i, (a, b) in enumerate(weights)
     ]
-    spread = []
-    for k, d in ((0, 1), (1, 0)):
-        for o in range(1, 4):
-            at = keys.at[y, x, c, k]
-            spread.append(remote(at, at, asem.at[0, k, o - 1], bsem.at[0, k, o - 1], device(d, o)))
     own = pltpu.make_async_copy(send.at[me], recv.at[0], psem)
     own.start()
     lax.fori_loop(1, 64, start, 0)
     for q in trades:
         q.start()
-    for q in spread:
-        q.start()
+    for q in fetches[7:]:
+        q.wait()
     for h in range(2):
         qc[h, :, 0:128] = qn[:, 128 * h : 128 * (h + 1)]
         qc[h, :, 128:256] = jnp.concatenate([qp[:, 64 * h : 64 * (h + 1)], zero], axis=1)
-    wkv[0:256, :] = wuv[...]
-    wkv[256:512, :] = wuk[...]
     own.wait()
 
     def arrive(k, _):
@@ -299,6 +322,11 @@
         rest = rest + dot(comb[1 + j], part, TN)
     own_out[:, 1536:2048] = (total[:, 1536:2048] + rest).astype(BF16)
     gathered[z, c] = own_out[...]
+    writes = [
+        pltpu.make_async_copy(a, b, osem.at[i])
+        for i, (a, b) in enumerate(((own_out, own_h), (dq_out, dq_h), (dp_out, dp_h)))
+    ]
+    writes[0].start()
     hops = [
         remote(own_out, gathered.at[z, c], gsem.at[o - 1], hsem.at[o - 1], device(2, o))
         for o in range(1, 4)
@@ -402,6 +430,8 @@
         val = (dqs[h] * SCALE).astype(BF16)
         dq_out[:, 128 * h : 128 * (h + 1)] = val[:, 0:128]
         dp_out[:, 64 * h : 64 * (h + 1)] = val[:, 128:192]
+    writes[1].start()
+    writes[2].start()
     settle(3)
 
     def close(r, _):
@@ -463,6 +493,8 @@
         for o in range(3):
             val = val + r3[k, o].astype(F32)
         out[48 * k : 48 * (k + 1), :] = val
+    for q in writes:
+        q.wait()
 
 
 def layer(*args):
@@ -483,9 +515,12 @@
             jax.ShapeDtypeStruct((256, 128), BF16),
             jax.ShapeDtypeStruct((144, 128), F32),
         ),
-        in_specs=[sm] + [vm] * 11 + [hbm] * 3,
-        out_specs=(vm, vm, vm, vm),
+        in_specs=[sm] + [hbm] * 14,
+        out_specs=(hbm, hbm, hbm, vm),
         scratch_shapes=[
+            room(6, 32, dtype=jnp.int32), room(6, 32, dtype=F32), room(32, 2048), room(32, 2048),
+            room(64, 256), room(256, 256), room(256, 128), room(256, 2048),
+            room(32, 2048), room(256, 256), room(256, 128),
             room(64, 8, 3072), room(64, 8, 3072),
             room(2, half, 2048), room(2, half, 2048), room(2, half, 2048),
             room(64, 8, 1536), room(64, 8, 1536),
@@ -496,6 +531,7 @@
             room(2, 3, 4, 4, 48, 128), room(3, 4, 4, 48, 128),
             room(3, 4, 4, 48, 128), room(3, 3, 4, 48, 128),
             room(3, 4, 48, 128), room(3, 3, 48, 128),
+            dma((12,)), dma((3,)), pltpu.SemaphoreType.REGULAR((2,)),
             dma((3,)), dma, dma((64,)), dma((64,)), dma((3,)), dma((3,)),
             dma((64,)), dma((64,)), dma((2, 2, 3)), dma((2, 2, 3)), dma((5,)), dma((5,)),
             dma((4,)), dma((4,)), dma((2, 3, 4)), dma((2, 3, 4)), dma((3,)), dma((3,)),
@@ -508,17 +544,42 @@
     )(*args)
 
 
+def lay_kernel(own, dq, dp, sums, own_out, dq_out, dp_out, lat_out, rope_out):
+    own_out[...] = own[...]
+    dq_out[...] = dq[...]
+    dp_out[...] = dp[...]
+    for l in range(4):
+        lat_out[:, 128 * l : 128 * (l + 1)] = sums[32 * l : 32 * (l + 1), :]
+    rope_out[0:16, :] = sums[128:144, 0:64]
+    rope_out[16:32, :] = sums[128:144, 64:128]
+
+
+def lay_out(*args):
+    vm = pl.BlockSpec(memory_space=pltpu.VMEM)
+    return pl.pallas_call(
+        lay_kernel,
+        out_shape=(
+            jax.ShapeDtypeStruct((32, 2048), BF16),
+            jax.ShapeDtypeStruct((256, 256), BF16),
+            jax.ShapeDtypeStruct((256, 128), BF16),
+            jax.ShapeDtypeStruct((32, 512), F32),
+            jax.ShapeDtypeStruct((32, 64), F32),
+        ),
+        in_specs=[vm] * 4,
+        out_specs=(vm,) * 5,
+    )(*args)
+
+
 def on_device(
     hidden, cotangent, routes, gates, offsets, w_gate, w_up, w_down, w_out,
     latent, rope_key, q_nope, q_pe, w_uk, w_uv,
 ):
-    resid_grad, dq, dpe, mine = layer(
-        offsets, routes.T, gates.T, hidden, cotangent, latent, rope_key, q_nope, q_pe,
-        w_uv, w_uk, w_out, w_gate[0].T, w_up[0].T, w_down[0],
+    return lay_out(
+        *layer(
+            offsets, routes.T, gates.T, hidden, cotangent, latent, rope_key.T, q_nope, q_pe,
+            w_uv, w_uk, w_out, w_gate[0].T, w_up[0].T, w_down[0],
+        )
     )
-    grad_latent = mine[:128].reshape(4, 32, 128).transpose(1, 0, 2).reshape(32, 512)
-    grad_rope = mine[128:].reshape(16, 2, 64).transpose(1, 0, 2).reshape(32, 64)
-    return (resid_grad, dq, dpe, grad_latent, grad_rope)
 
 
 def solution(mesh):

time: 145 us -> 130 us (0.90)
  local copies, waits for them, and re-layouts: 8.97 us -> 0 us
  Pallas kernels: 135 us -> 129 us
    pallas_call x1, Pallas kernels: 135 us -> 127 us  [layer(): pl.pallas_call(layer_kernel, out_shape=(jax.ShapeDtypeStruct((32, 2048),...]
    unnamed x4 -> x0, local copies, waits for them, and re-layouts: 6.1 us -> none
    pallas_call x0 -> x1, Pallas kernels: none -> 1.8 us  [lay_out(): pl.pallas_call(lay_kernel, out_shape=(jax.ShapeDtypeStruct((32, 2048), BF...]
    slice x2 -> x0, local copies, waits for them, and re-layouts: 1.54 us -> none  [the longest x1 0.85 us: on_device(): mine[:128].reshape(4, 32, 128).transpose(1, 0, 2).reshape(32, 512)]
where the time goes in v2:
time: 130 us; the launch traced here: 129 us
  Pallas kernels  129 us (99%)
    pallas_call x1, Pallas kernels, layer(): pl.pallas_call(layer_kernel, out_shape=(jax.ShapeDtypeStruct((32, 2048),...  127 us

profile of v2, /device:TPU:0, one launch (start us, length us, event | category | flops | bytes accessed | tf_op | source)
XLA Modules:
  0.0 129.4 jit_solution(585280713014185145)
XLA Ops:
  0.6 127.0 %shard_map.182 = (bf16[32,2048]{1,0:T(8,128)(2,1)}, bf16[256,256]{1,0:T(8,128)(2,1)}, bf16[256,128]{1,0:T(8,128)(2,1)}, f32[144,128]{1,0:T(8,128)}) custom-call(s32[16]{0:T(128)} %offs.1, s32[6,32]{1,0:T(8,128)} %bitcast.14, f32[6,32]{1,0:T(8,128)} %bitcast.15, bf16[32,2048]{1,0:T(8,128)(2,1)} %hid_h.1, bf16[32,2048]{1,0:T(8,128)(2,1)} %cot_h.1, ...), custom_call_target="tpu_custom_call" | custom-call | flops 22000001024 | bytes 20000000 | tf_op jit(solution)/shard_map/pallas_call | solution.py:510
  127.6 1.8 %shard_map.183 = (bf16[32,2048]{1,0:T(8,128)(2,1)}, bf16[256,256]{1,0:T(8,128)(2,1)}, bf16[256,128]{1,0:T(8,128)(2,1)}, f32[32,512]{1,0:T(8,128)}, f32[32,64]{1,0:T(8,128)}) custom-call(bf16[32,2048]{1,0:T(8,128)(2,1)} %get-tuple-element.9.own, bf16[256,256]{1,0:T(8,128)(2,1)} %get-tuple-element.10.dq, bf16[256,128]{1,0:T(8,128)(2,1)} %get-tuple-element.11.dp, ...), custom_call_target="tpu_custom_call" | custom-call | tf_op jit(solution)/shard_map/pallas_call | solution.py:559

commit v3 on v2

--- a/solution.py
+++ b/solution.py
@@ -84,7 +84,7 @@
     rt, gt, hid, cot, rope, qn, qp, wout, own_out, dq_out, dp_out,
     send, recv, wgb, wub, wdb, back, landed, keys, gathered, comb, xs, dys, sc,
     wkv, qc, gx, dd, terms, r0, r1, ry, a1, r2, a2, r3,
-    fsem, osem, sync, lsem, psem, ssem, rsem, wssem, wrsem, bssem, brsem, asem, bsem, gsem, hsem,
+    fsem, osem, sync, lsem, psem, ssem, rsem, wssem, wrsem, bssem, brsem, asem, bsem, gsem, hsem, psem2, qsem2,
     s0, t0, s1, t1, sy, ty, ss, rs,
 ):
     y, x, z, c = place()
@@ -305,10 +305,12 @@
 
     def ret_finish(k, _):
         pc = peer(k)[0]
+        remote(back.at[k], landed.at[pc], bssem.at[k], brsem.at[pc], partner).wait_recv()
+        return 0
+
+    def sent(k, _):
         remote(send.at[0], recv.at[k], ssem.at[k], rsem.at[k], partner).wait_send()
-        q = remote(back.at[k], landed.at[pc], bssem.at[k], brsem.at[pc], partner)
-        q.wait_send()
-        q.wait_recv()
+        remote(back.at[k], landed.at[me], bssem.at[k], brsem.at[me], partner).wait_send()
         return 0
 
     lax.fori_loop(1, 64, ret_finish, 0)
@@ -333,11 +335,17 @@
     ]
     for q in hops:
         q.start()
-    for q in hops:
-        q.wait()
-    last = remote(gathered.at[:, c], gathered.at[:, c], gsem.at[3], hsem.at[3], partner)
-    last.start()
-    last.wait()
+
+    def pair(o):
+        at = gathered.at[(z + 4 - o) % 4, c]
+        return remote(at, at, psem2.at[o], qsem2.at[o], partner)
+
+    pair(0).start()
+    for o in range(1, 4):
+        hops[o - 1].wait()
+        pair(o).start()
+    for o in range(4):
+        pair(o).wait()
 
     go = dot(gathered[...].reshape(256, 2048), wout[...], NT).astype(BF16).astype(F32)
     lane = iota((256, 128), 1)
@@ -465,7 +473,7 @@
 
     lax.fori_loop(0, 16, add1, 0)
 
-    def stage(i, src, dst):
+    def stage(i, src, dst, beside=None):
         copies = []
         for o in range(1, 4):
             for k in range(3):
@@ -478,10 +486,12 @@
                 )
         for q in copies:
             q.start()
+        if beside:
+            beside()
         for q in copies:
             q.wait()
 
-    stage(1, a1, r2)
+    stage(1, a1, r2, lambda: lax.fori_loop(1, 64, sent, 0))
     for k in range(3):
         val = a1[k, coord[ORDERS[k][1]]].astype(F32)
         for o in range(3):
@@ -533,7 +543,7 @@
             room(3, 4, 48, 128), room(3, 3, 48, 128),
             dma((12,)), dma((3,)), pltpu.SemaphoreType.REGULAR((2,)),
             dma((3,)), dma, dma((64,)), dma((64,)), dma((3,)), dma((3,)),
-            dma((64,)), dma((64,)), dma((2, 2, 3)), dma((2, 2, 3)), dma((5,)), dma((5,)),
+            dma((64,)), dma((64,)), dma((2, 2, 3)), dma((2, 2, 3)), dma((5,)), dma((5,)), dma((4,)), dma((4,)),
             dma((4,)), dma((4,)), dma((2, 3, 4)), dma((2, 3, 4)), dma((3,)), dma((3,)),
             dma((2, 3, 3)), dma((2, 3, 3)),
         ],

time: 130 us -> 129 us (level)
  no operation moved by 1% of the time
where the time goes in v3:
time: 129 us
  Pallas kernels  128 us (99%)
    pallas_call x1, Pallas kernels, layer(): pl.pallas_call(layer_kernel, out_shape=(jax.ShapeDtypeStruct((32, 2048),...  126 us

profile of v3, /device:TPU:0, one launch (start us, length us, event | category | flops | bytes accessed | tf_op | source)
XLA Modules:
  0.0 128.8 jit_solution(6546463185689386788)
XLA Ops:
  0.6 126.4 %shard_map.182 = (bf16[32,2048]{1,0:T(8,128)(2,1)}, bf16[256,256]{1,0:T(8,128)(2,1)}, bf16[256,128]{1,0:T(8,128)(2,1)}, f32[144,128]{1,0:T(8,128)}) custom-call(s32[16]{0:T(128)} %offs.1, s32[6,32]{1,0:T(8,128)} %bitcast.14, f32[6,32]{1,0:T(8,128)} %bitcast.15, bf16[32,2048]{1,0:T(8,128)(2,1)} %hid_h.1, bf16[32,2048]{1,0:T(8,128)(2,1)} %cot_h.1, ...), custom_call_target="tpu_custom_call" | custom-call | flops 22000001024 | bytes 20000000 | tf_op jit(solution)/shard_map/pallas_call | solution.py:520
  127.0 1.8 %shard_map.183 = (bf16[32,2048]{1,0:T(8,128)(2,1)}, bf16[256,256]{1,0:T(8,128)(2,1)}, bf16[256,128]{1,0:T(8,128)(2,1)}, f32[32,512]{1,0:T(8,128)}, f32[32,64]{1,0:T(8,128)}) custom-call(bf16[32,2048]{1,0:T(8,128)(2,1)} %get-tuple-element.9.own, bf16[256,256]{1,0:T(8,128)(2,1)} %get-tuple-element.10.dq, bf16[256,128]{1,0:T(8,128)(2,1)} %get-tuple-element.11.dp, ...), custom_call_target="tpu_custom_call" | custom-call | tf_op jit(solution)/shard_map/pallas_call | solution.py:569

commit v4 on v3

--- a/solution.py
+++ b/solution.py
@@ -180,7 +180,7 @@
     ]
     own = pltpu.make_async_copy(send.at[me], recv.at[0], psem)
     own.start()
-    lax.fori_loop(1, 64, start, 0)
+    lax.fori_loop(1, 64, start, 0, unroll=3)
     for q in trades:
         q.start()
     for q in fetches[7:]:
@@ -304,7 +304,7 @@
     own.wait()
 
     def ret_finish(k, _):
-        pc = peer(k)[0]
+        pc = (me + k) % 64
         remote(back.at[k], landed.at[pc], bssem.at[k], brsem.at[pc], partner).wait_recv()
         return 0
 
@@ -313,7 +313,7 @@
         remote(back.at[k], landed.at[me], bssem.at[k], brsem.at[me], partner).wait_send()
         return 0
 
-    lax.fori_loop(1, 64, ret_finish, 0)
+    lax.fori_loop(1, 64, ret_finish, 0, unroll=3)
 
     total = cot[...].astype(F32)
     rest = jnp.zeros((32, 512), F32)

time: 129 us -> 129 us (level)
  no operation moved by 1% of the time
where the time goes in v4:
time: 129 us
  Pallas kernels  128 us (99%)
    pallas_call x1, Pallas kernels, layer(): pl.pallas_call(layer_kernel, out_shape=(jax.ShapeDtypeStruct((32, 2048),...  126 us

profile of v4, /device:TPU:0, one launch (start us, length us, event | category | flops | bytes accessed | tf_op | source)
XLA Modules:
  0.0 128.8 jit_solution(17503246762715652910)
XLA Ops:
  0.6 126.3 %shard_map.182 = (bf16[32,2048]{1,0:T(8,128)(2,1)}, bf16[256,256]{1,0:T(8,128)(2,1)}, bf16[256,128]{1,0:T(8,128)(2,1)}, f32[144,128]{1,0:T(8,128)}) custom-call(s32[16]{0:T(128)} %offs.1, s32[6,32]{1,0:T(8,128)} %bitcast.14, f32[6,32]{1,0:T(8,128)} %bitcast.15, bf16[32,2048]{1,0:T(8,128)(2,1)} %hid_h.1, bf16[32,2048]{1,0:T(8,128)(2,1)} %cot_h.1, ...), custom_call_target="tpu_custom_call" | custom-call | flops 22000001024 | bytes 20000000 | tf_op jit(solution)/shard_map/pallas_call | solution.py:520
  127.0 1.8 %shard_map.183 = (bf16[32,2048]{1,0:T(8,128)(2,1)}, bf16[256,256]{1,0:T(8,128)(2,1)}, bf16[256,128]{1,0:T(8,128)(2,1)}, f32[32,512]{1,0:T(8,128)}, f32[32,64]{1,0:T(8,128)}) custom-call(bf16[32,2048]{1,0:T(8,128)(2,1)} %get-tuple-element.9.own, bf16[256,256]{1,0:T(8,128)(2,1)} %get-tuple-element.10.dq, bf16[256,128]{1,0:T(8,128)(2,1)} %get-tuple-element.11.dp, ...), custom_call_target="tpu_custom_call" | custom-call | tf_op jit(solution)/shard_map/pallas_call | solution.py:569
